TPU v7x, 256 devices: a whole 4x4x8 slice. The times are simulated.
256 devices in a mesh: dp: 16 (over z, x_lo), seq: 16 (over y, x_hi, core).
Axes of the slice: x: 4 (x_hi: 2, x_lo: 2; x = x_hi * 2 + x_lo), y: 4, z: 8, core: 2. Of those that a mesh axis runs over, the one named last changes fastest.
Arguments:
- frames: bfloat16 [16, 4096, 1536], P('dp', 'seq'), may hold values from -0.29882812 to 0.29882812
- segment_ids: int32 [16, 4096], P('dp', 'seq'), may hold values from 0 to 11, never falling along the last dimension, each value on 1 to 3072 neighbouring positions
- ln_attn_gain: float32 [1536], replicated, may hold values from 0.25 to 1.75
- w_qkv: bfloat16 [1536, 2304], P('dp'), as said below
- w_out: bfloat16 [768, 1536], P('dp'), may hold values from -0.21875 to 0.21875
- ln_conv_gain: float32 [1536], replicated, may hold values from 0.25 to 1.75
- w_glu: bfloat16 [1536, 3072], P('dp'), may hold values from -0.15625 to 0.15625
- dw_kernel: float32 [32, 1536], replicated, may hold values from -1 to 1
- ln_mid_gain: float32 [1536], replicated, may hold values from 0.25 to 1.75
Outputs:
- block_out: bfloat16 [16, 4096, 1536], P('dp', 'seq')
Inputs may be any that keep to these rules, and one draw needn't show every extreme that they name: `segment_ids`: within each stream the ids start at 0 and never fall; each utterance has 1 to 3072 frames and one has exactly 3072. `w_qkv`: a projection matrix with independent entries.
All inputs are finite; a program needn't handle non-finite values.
Results may differ from a plain program's by a relative error of at most 0.025.
The roundings to bfloat16 on the way count: a program that leaves them out, or rounds other values in their place, can miss the bound.
Values may be sent and summed in bfloat16 or wider, within the bound.
No kernel may reach another device: no remote copies, remote signals or barrier semaphores. Data moves between devices by JAX's collectives and lax.ppermute only.
A program may use at most 192 MiB of HBM per device.

v0:
```python
import math
import jax
import jax.numpy as jnp
from jax import lax
from jax.sharding import PartitionSpec as P

D = 1536
HEADS = 12
HD = 64
CONV_K = 32


def with_halo(block, sides, width):
    for axis, dim in sides:
        count = lax.axis_size(axis)
        forward = [(i, i + 1) for i in range(count - 1)]
        backward = [(target, source) for source, target in forward]
        low = lax.ppermute(
            lax.slice_in_dim(block, block.shape[dim] - width, None, axis=dim), axis, forward
        )
        high = lax.ppermute(lax.slice_in_dim(block, 0, width, axis=dim), axis, backward)
        block = jnp.concatenate([low, block, high], axis=dim)
    return block


def layer_norm(values, gain):
    values = values.astype(jnp.float32)
    centre = jnp.mean(values, -1, keepdims=True)
    spread = jnp.mean((values - centre) ** 2, -1, keepdims=True)
    return (values - centre) * lax.rsqrt(spread + 1e-05) * gain


def add_rows(left, block_rows):
    return jnp.dot(left, block_rows, preferred_element_type=jnp.float32)


def body(
    frames, segment_ids, ln_attn_gain, w_qkv, w_out, ln_conv_gain, w_glu, dw_kernel, ln_mid_gain
):
    width = HEADS * HD
    local = frames[0]
    frame_count = local.shape[0]
    local_segs = segment_ids[0]
    shard_index = lax.axis_index("seq")
    first_frame = shard_index * frame_count
    all_segs = lax.all_gather(segment_ids, "seq", axis=1, tiled=True)[0]
    normed = layer_norm(local, ln_attn_gain).astype(jnp.bfloat16)
    projected = add_rows(normed, lax.all_gather(w_qkv, "dp", axis=0, tiled=True))
    projected = projected.astype(jnp.bfloat16)
    queries = projected[:, :width].reshape(frame_count, HEADS, HD)
    keys_local = projected[:, width : 2 * width]
    values_local = projected[:, 2 * width :]
    inverse_root = 1.0 / math.sqrt(HD)
    keys_part = lax.all_gather(keys_local, "seq", axis=0, tiled=True)
    values_part = lax.all_gather(values_local, "seq", axis=0, tiled=True)
    rows = keys_part.shape[0]
    running = jnp.full((HEADS, frame_count), -1e30, jnp.float32)
    scores = (
        jnp.einsum(
            "qhd,khd->hqk",
            queries,
            keys_part.reshape(rows, HEADS, HD),
            preferred_element_type=jnp.float32,
        )
        * inverse_root
    )
    same_seg = (local_segs[:, None] == all_segs[None, :])[None]
    scores = jnp.where(same_seg, scores, -1e30)
    newest = jnp.maximum(running, jnp.max(scores, -1))
    raised = jnp.where(same_seg, jnp.exp(scores - newest[:, :, None]), 0.0)
    totals = jnp.sum(raised, -1)
    product = jnp.einsum(
        "hqk,khd->qhd",
        raised.astype(jnp.bfloat16),
        values_part.reshape(rows, HEADS, HD),
        preferred_element_type=jnp.float32,
    )
    summed = product
    running, totals, summed = (newest, totals, summed.reshape(frame_count, width))
    attended = (
        (summed.reshape(frame_count, HEADS, HD) / jnp.transpose(totals)[:, :, None])
        .reshape(frame_count, width)
        .astype(jnp.bfloat16)
    )
    attn = add_rows(attended, lax.all_gather(w_out, "dp", axis=0, tiled=True))
    resid = (local.astype(jnp.float32) + attn).astype(jnp.bfloat16)
    glu_in = layer_norm(resid, ln_conv_gain).astype(jnp.bfloat16)
    glu_out = add_rows(glu_in, lax.all_gather(w_glu, "dp", axis=0, tiled=True))
    gated = (glu_out[:, :D] * jax.nn.sigmoid(glu_out[:, D:])).astype(jnp.bfloat16)
    half_taps = CONV_K // 2
    widened = with_halo(gated, (("seq", 0),), half_taps)
    padded_segs = jnp.pad(all_segs, (half_taps, half_taps), constant_values=-1)
    rim_segs = lax.dynamic_slice_in_dim(padded_segs, first_frame, frame_count + 2 * half_taps)
    conv = jnp.zeros((frame_count, D), jnp.float32)
    for tap_index in range(CONV_K):
        keep = (rim_segs[tap_index : tap_index + frame_count] == local_segs)[:, None]
        shifted = widened[tap_index : tap_index + frame_count].astype(jnp.float32)
        conv = conv + jnp.where(keep, shifted * dw_kernel[tap_index], 0.0)
    middle = layer_norm(conv, ln_mid_gain)
    result = (resid.astype(jnp.float32) + middle * jax.nn.sigmoid(middle)).astype(jnp.bfloat16)
    return result[None]


def solution(mesh):
    return jax.shard_map(
        body,
        mesh=mesh,
        in_specs=(
            P("dp", "seq", None),
            P("dp", "seq"),
            P(),
            P("dp", None),
            P("dp", None),
            P(),
            P("dp", None),
            P(),
            P(),
        ),
        out_specs=P("dp", "seq", None),
        check_vma=False,
    )
```

profile of v0, /device:TPU:39, one launch (start us, length us, event | category | flops | bytes accessed | tf_op | source)
XLA Modules:
  0.0 635.7 jit_solution(8516103408520678854)
XLA Ops:
  6.5 0.7 all-gather.6.cloned.1.call-update
  7.3 1.3 convert_reduce_fusion
  9.0 159.5 %all-gather.6.cloned.1.call-done = bf16[1536,2304]{1,0:T(8,128)(2,1)} async-done(((bf16[96,2304]{1,0:T(8,128)(2,1)}), bf16[1536,2304]{1,0:T(8,128)(2,1)}) %all-gather.6.cloned.1.call-update) | async-done | bytes 7077904 | tf_op jit(solution)/shard_map/all_gather | solution.py:48
  168.5 5.1 convolution_convert_fusion
  173.6 1.0 fusion.70
  174.7 0.7 all-gather.8.cloned.1.call-update
  176.0 0.5 all-gather.14.cloned.1.call-update
  176.6 22.1 %all_gather.22 = s32[1,4096]{1,0:T(1,128)S(1)} all-gather(s32[1,256]{1,0:T(1,128)S(1)} %copy-done.2), channel_id=1, replica_groups=mesh['dp'=16,'seq'=16] {'seq'}, dimensions={1}, use_global_device_ids=true | all-gather | bytes 17408 | tf_op jit(solution)/shard_map/all_gather | solution.py:46
  199.2 0.6 broadcast_compare_fusion
  200.0 43.1 %all-gather.10.cloned.1.call-done = bf16[4096,768]{1,0:T(8,128)(2,1)} async-done(((bf16[256,768]{1,0:T(8,128)(2,1)}), bf16[4096,768]{1,0:T(8,128)(2,1)}) %all-gather.10.cloned.1.call-update) | async-done | bytes 6291472 | tf_op jit(solution)/shard_map/all_gather | solution.py:54
  243.1 8.6 %copy.15 = bf16[4096,768]{0,1:T(8,128)(2,1)} copy(bf16[4096,768]{1,0:T(8,128)(2,1)} %all-gather.10.cloned.1.call-done) | data formatting | bytes 12582912 | tf_op jit(solution)/shard_map/all_gather | solution.py:54
  251.7 61.2 %all-gather.8.cloned.1.call-done = bf16[4096,768]{1,0:T(8,128)(2,1)} async-done(((bf16[256,768]{1,0:T(8,128)(2,1)}), bf16[4096,768]{1,0:T(8,128)(2,1)}) %all-gather.8.cloned.1.call-update) | async-done | bytes 6291472 | tf_op jit(solution)/shard_map/all_gather | solution.py:55
  312.9 8.7 %copy.13 = bf16[4096,768]{0,1:T(8,128)(2,1)} copy(bf16[4096,768]{1,0:T(8,128)(2,1)} %all-gather.8.cloned.1.call-done) | data formatting | bytes 12582912 | tf_op jit(solution)/shard_map/all_gather | solution.py:55
  321.6 23.4 %fusion = (f32[12,256]{1,0:T(8,128)S(1)}, f32[12,256,4096]{2,1,0:T(8,128)}) fusion(pred[256,4096]{1,0:T(8,128)(4,1)S(1)} %broadcast_compare_fusion, bf16[256,12,64]{0,2,1:T(8,128)(2,1)S(1)} %bitcast.41, bf16[4096,12,64]{0,2,1:T(8,128)(2,1)} %bitcast.39), kind=kOutput, calls=%fused_computation.2 | convolution fusion | flops 1648358400 | bytes 58077184 | tf_op jit(solution)/shard_map/qhd,khd->hqk/dot_general | solution.py:59
  345.0 23.5 %fusion.1 = f32[12,256]{1,0:T(8,128)S(1)} fusion(f32[12,256,4096]{2,1,0:T(8,128)} %get-tuple-element.77, f32[12,256]{1,0:T(8,128)S(1)} %broadcast_maximum_fusion, pred[256,4096]{1,0:T(8,128)(4,1)S(1)} %broadcast_compare_fusion), kind=kLoop, calls=%fused_computation.3 | loop fusion | flops 62911488 | bytes 51404800 | tf_op jit(solution)/shard_map/reduce_sum | solution.py:71
  368.5 21.7 %fusion.25 = bf16[256,12,64]{0,2,1:T(8,128)(2,1)S(1)} fusion(bf16[4096,12,64]{0,2,1:T(8,128)(2,1)} %bitcast.40, f32[12,256,4096]{2,1,0:T(8,128)} %get-tuple-element.77, f32[12,256]{1,0:T(8,128)S(1)} %broadcast_maximum_fusion, pred[256,4096]{1,0:T(8,128)(4,1)S(1)} %broadcast_compare_fusion, f32[256,12]{0,1:T(8,128)S(1)} %bitcast.45), kind=kOutput, calls=%fused_computation.62 | convolution fusion | flops 1673920512 | bytes 58089472 | tf_op jit(solution)/shard_map/hqk,khd->qhd/dot_general | solution.py:72
  390.2 2.5 fusion.72
  393.1 199.7 %all-gather.14.cloned.1.call-done = bf16[1536,3072]{1,0:T(8,128)(2,1)} async-done(((bf16[96,3072]{1,0:T(8,128)(2,1)}), bf16[1536,3072]{1,0:T(8,128)(2,1)}) %all-gather.14.cloned.1.call-update) | async-done | bytes 9437200 | tf_op jit(solution)/shard_map/all_gather | solution.py:88
  592.8 5.3 fusion.28
  598.5 4.7 collective-permute-start
  603.2 1.9 collective-permute-start.1
  605.4 5.7 collective-permute-done.1
  611.0 16.3 %fusion.69 = (f32[256]{0:T(256)S(1)}, f32[256,1536]{1,0:T(8,128)S(1)}) fusion(f32[1536]{0:T(1024)S(1)} %get-tuple-element.35, bf16[16,1536]{1,0:T(8,128)(2,1)S(1)} %collective-permute-done.1, bf16[256,1536]{1,0:T(8,128)(2,1)S(1)} %fusion.18, pred[256]{0:T(512)(128)(4,1)S(1)} %get-tuple-element.45, f32[1536]{0:T(1024)S(1)} %get-tuple-element.36, ...), kind=kLoop, calls=%fused_computation.195 | loop fusion | flops 86900480 | bytes 2663424 | tf_op jit(solution)/shard_map/reduce_sum | solution.py:28
  627.6 1.5 fusion.65
  (39 shorter events, 3.1 us)
Async XLA Ops:
  6.5 2.1 copy-start
  6.5 161.9 %copy-start.4 = (f32[1536]{0:T(1024)S(1)}, f32[1536]{0:T(1024)}, u32[]{:S(2)}) copy-start(f32[1536]{0:T(1024)} %param.11) | copy-start | bytes 18436
  6.5 161.9 %all-gather.6.cloned.1.call-start = ((), (), s32[]{:S(2)}) async-start(), calls=%async_computation | async-start | bytes 7520256 | tf_op jit(solution)/shard_map/all_gather | solution.py:48
  7.3 235.9 %all-gather.10.cloned.1.call-start = ((), (), s32[]{:S(2)}) async-start(), calls=%async_computation.2 | async-start | bytes 6684672 | tf_op jit(solution)/shard_map/all_gather | solution.py:54
  173.6 2.9 copy-start.2
  173.6 25.1 %copy-start.1 = (f32[32,1536]{1,0:T(8,128)S(1)}, f32[32,1536]{1,0:T(8,128)}, u32[]{:S(2)}) copy-start(f32[32,1536]{1,0:T(8,128)} %param.16) | copy-start | bytes 589828
  174.6 138.3 %all-gather.8.cloned.1.call-start = ((), (), s32[]{:S(2)}) async-start(), calls=%async_computation.1 | async-start | bytes 6684672 | tf_op jit(solution)/shard_map/all_gather | solution.py:55
  175.4 214.9 %all-gather.12.cloned.1.call-start = ((), (), s32[]{:S(2)}) async-start(), calls=%async_computation.3 | async-start | bytes 2506752 | tf_op jit(solution)/shard_map/all_gather | solution.py:85
  175.9 416.8 %all-gather.14.cloned.1.call-start = ((), (), s32[]{:S(2)}) async-start(), calls=%async_computation.4 | async-start | bytes 10027008 | tf_op jit(solution)/shard_map/all_gather | solution.py:88
  392.8 200.0 %copy-start.5 = (f32[1536]{0:T(1024)S(1)}, f32[1536]{0:T(1024)}, u32[]{:S(2)}) copy-start(f32[1536]{0:T(1024)} %param.14) | copy-start | bytes 18436
  598.5 6.9 %collective-permute-start = (bf16[16,1536]{1,0:T(8,128)(2,1)S(1)}, bf16[16,1536]{1,0:T(8,128)(2,1)S(1)}, u32[]{:S(2)}, u32[]{:S(2)}) collective-permute-start(bf16[16,1536]{1,0:T(8,128)(2,1)S(1)} %get-tuple-element.42), channel_id=1, source_target_pairs={{0,1},{1,2},{2,3},{3,4},{4,5},{5,6},{6,7},{7,8},{8,9},{9,10},{10,1... | collective-permute-start | bytes 147464 | tf_op jit(solution)/shard_map/ppermute | solution.py:18
  603.2 7.8 %collective-permute-start.1 = (bf16[16,1536]{1,0:T(8,128)(2,1)S(1)}, bf16[16,1536]{1,0:T(8,128)(2,1)S(1)}, u32[]{:S(2)}, u32[]{:S(2)}) collective-permute-start(bf16[16,1536]{1,0:T(8,128)(2,1)S(1)} %get-tuple-element.43), channel_id=1, source_target_pairs={{1,0},{2,1},{3,2},{4,3},{5,4},{6,5},{7,6},{8,7},{9,8},{10,9},{11,1... | collective-permute-start | bytes 147464 | tf_op jit(solution)/shard_map/ppermute | solution.py:21
  611.0 16.6 %copy-start.3 = (f32[1536]{0:T(1024)S(1)}, f32[1536]{0:T(1024)}, u32[]{:S(2)}) copy-start(f32[1536]{0:T(1024)} %param.17) | copy-start | bytes 18436
Sparse Core Ops, SparseCore 0:
  9.1 159.2 all-gather.5
  174.8 68.3 all-gather.9
  245.9 66.9 all-gather.7
  314.6 64.0 all-gather.11
  380.3 212.4 all-gather.13
where the time goes:
time: 637 us; the launch traced here: 636 us
  waiting for transfers between devices  472 us (74%)
  matrix products  58 us (9%)
  other arithmetic  44.8 us (7%)
  blocking collectives  22.1 us (3%)
  local copies, waits for them, and re-layouts  19.1 us (3%)
  between operations  13.3 us (2%)
  starting transfers between devices  6.79 us (1%)
    all_gather x1, waiting for transfers between devices, body(): glu_out = add_rows(glu_in, lax.all_gather(w_glu, 'dp', axis=0, tiled=True))  200 us
    all_gather x1, waiting for transfers between devices, body(): lax.all_gather(w_qkv, 'dp', axis=0, tiled=True)  159 us
    all_gather x1, waiting for transfers between devices, body(): values_part = lax.all_gather(values_local, 'seq', axis=0, tiled=True)  61.2 us
    all_gather x1, waiting for transfers between devices, body(): keys_part = lax.all_gather(keys_local, 'seq', axis=0, tiled=True)  43.1 us
    reduce_sum x1, other arithmetic, body(): totals = jnp.sum(raised, -1)  23.5 us
    dot_general x1, matrix products, body(): jnp.einsum('qhd,khd->hqk', queries, keys_part.reshape(rows, HEADS, HD), p...  23.4 us
    all_gather x1, blocking collectives, body(): all_segs = lax.all_gather(segment_ids, 'seq', axis=1, tiled=True)[0]  22.1 us
    dot_general x1, matrix products, body(): jnp.einsum('hqk,khd->qhd', raised.astype(jnp.bfloat16), values_part.resha...  21.7 us
  transfers between devices with their start and end apart: 7, of which 5 were waited for; matrix products, arithmetic and copies ran while one was open for 14% of the time, Pallas kernels for 0%

commit v1 on v0

--- a/solution.py
+++ b/solution.py
@@ -51,8 +51,13 @@
     keys_local = projected[:, width : 2 * width]
     values_local = projected[:, 2 * width :]
     inverse_root = 1.0 / math.sqrt(HD)
-    keys_part = lax.all_gather(keys_local, "seq", axis=0, tiled=True)
-    values_part = lax.all_gather(values_local, "seq", axis=0, tiled=True)
+    keys_part, values_part = jnp.split(
+        lax.all_gather(
+            jnp.concatenate([keys_local, values_local], axis=1), "seq", axis=0, tiled=True
+        ),
+        [keys_local.shape[1]],
+        axis=1,
+    )
     rows = keys_part.shape[0]
     running = jnp.full((HEADS, frame_count), -1e30, jnp.float32)
     scores = (

time: 637 us -> 594 us (0.932)
  waiting for transfers between devices: 472 us -> 412 us
  local copies, waits for them, and re-layouts: 19.1 us -> 31.5 us
    all_gather x2 -> x1, waiting for transfers between devices: 104 us -> 69.3 us  [body(): lax.all_gather(jnp.concatenate([keys_local, values_local], axis=1), 'seq'...]
    split x0 -> x3, local copies, waits for them, and re-layouts: none -> 27.7 us  [body(): jnp.split(lax.all_gather(jnp.concatenate([keys_local, values_local], axis...]
    all_gather x1, waiting for transfers between devices: 200 us -> 181 us  [body(): glu_out = add_rows(glu_in, lax.all_gather(w_glu, 'dp', axis=0, tiled=True))]
    all_gather x2 -> x0, local copies, waits for them, and re-layouts: 17.3 us -> none  [the longest x1 8.7 us: body(): values_part = lax.all_gather(values_local, 'seq', axis=0, tiled=True)]
  transfers between devices with their start and end apart: 7 -> 6, of which waited for: 5 -> 4; matrix products, arithmetic and copies ran while one was open for 14% -> 18% of each run, Pallas kernels for 0% -> 0%
where the time goes in v1:
time: 594 us; the launch traced here: 590 us
  waiting for transfers between devices  412 us (69%)
  matrix products  58.2 us (10%)
  other arithmetic  44.8 us (8%)
  local copies, waits for them, and re-layouts  31.5 us (5%)
  blocking collectives  22.1 us (4%)
  between operations  13.3 us (2%)
  starting transfers between devices  8.09 us (1%)
    all_gather x1, waiting for transfers between devices, body(): glu_out = add_rows(glu_in, lax.all_gather(w_glu, 'dp', axis=0, tiled=True))  181 us
    all_gather x1, waiting for transfers between devices, body(): lax.all_gather(w_qkv, 'dp', axis=0, tiled=True)  159 us
    all_gather x1, waiting for transfers between devices, body(): lax.all_gather(jnp.concatenate([keys_local, values_local], axis=1), 'seq'...  69.3 us
    split x3, local copies, waits for them, and re-layouts, body(): jnp.split(lax.all_gather(jnp.concatenate([keys_local, values_local], axis...  27.7 us
    reduce_sum x1, other arithmetic, body(): totals = jnp.sum(raised, -1)  23.4 us
    dot_general x1, matrix products, body(): jnp.einsum('qhd,khd->hqk', queries, keys_part.reshape(rows, HEADS, HD), p...  23.4 us
    all_gather x1, blocking collectives, body(): all_segs = lax.all_gather(segment_ids, 'seq', axis=1, tiled=True)[0]  22.1 us
    dot_general x1, matrix products, body(): jnp.einsum('hqk,khd->qhd', raised.astype(jnp.bfloat16), values_part.resha...  21.8 us
  transfers between devices with their start and end apart: 6, of which 4 were waited for; matrix products, arithmetic and copies ran while one was open for 18% of the time, Pallas kernels for 0%

profile of v1, /device:TPU:39, one launch (start us, length us, event | category | flops | bytes accessed | tf_op | source)
XLA Modules:
  0.0 590.2 jit_solution(7065058141874805537)
XLA Ops:
  6.5 0.7 all-gather.5.cloned.1.call-update
  7.3 1.3 convert_reduce_fusion
  9.0 159.5 %all-gather.5.cloned.1.call-done = bf16[1536,2304]{1,0:T(8,128)(2,1)} async-done(((bf16[96,2304]{1,0:T(8,128)(2,1)}), bf16[1536,2304]{1,0:T(8,128)(2,1)}) %all-gather.5.cloned.1.call-update) | async-done | bytes 7077904 | tf_op jit(solution)/shard_map/all_gather | solution.py:48
  168.5 5.1 convolution_convert_fusion
  173.6 1.1 copy-done.1
  174.7 0.9 concatenate.42
  175.7 0.7 all-gather.9.cloned.1.call-update
  177.0 22.1 %all_gather.19 = s32[1,4096]{1,0:T(1,128)S(1)} all-gather(s32[1,256]{1,0:T(1,128)S(1)} %copy-done.3), channel_id=1, replica_groups=mesh['dp'=16,'seq'=16] {'seq'}, dimensions={1}, use_global_device_ids=true | all-gather | bytes 17408 | tf_op jit(solution)/shard_map/all_gather | solution.py:46
  200.3 1.0 slice.434
  201.5 69.3 %all-gather.7.cloned.1.call-done = bf16[4096,1536]{1,0:T(8,128)(2,1)} async-done(((bf16[256,1536]{1,0:T(8,128)(2,1)}), bf16[4096,1536]{1,0:T(8,128)(2,1)}) %all-gather.7.cloned.1.call-update) | async-done | bytes 12582928 | tf_op jit(solution)/shard_map/all_gather | solution.py:55
  270.8 10.3 %fusion.70 = (bf16[4096,768]{1,0:T(8,128)(2,1)}, bf16[4096,768]{1,0:T(8,128)(2,1)}) fusion(bf16[4096,1536]{1,0:T(8,128)(2,1)} %all-gather.7.cloned.1.call-done), kind=kLoop, calls=%fused_computation.196 | loop fusion | bytes 25165824 | tf_op jit(solution)/shard_map/split | solution.py:54
  281.1 8.6 %copy.13 = bf16[4096,768]{0,1:T(8,128)(2,1)} copy(bf16[4096,768]{1,0:T(8,128)(2,1)} %get-tuple-element.40) | data formatting | bytes 12582912 | tf_op jit(solution)/shard_map/split | solution.py:54
  289.7 8.7 %copy.15 = bf16[4096,768]{0,1:T(8,128)(2,1)} copy(bf16[4096,768]{1,0:T(8,128)(2,1)} %get-tuple-element.39) | data formatting | bytes 12582912 | tf_op jit(solution)/shard_map/split | solution.py:54
  298.5 23.4 %fusion = (f32[12,256]{1,0:T(8,128)S(1)}, f32[12,256,4096]{2,1,0:T(8,128)}) fusion(pred[256,4096]{1,0:T(8,128)(4,1)S(1)} %broadcast_compare_fusion, bf16[256,12,64]{0,2,1:T(8,128)(2,1)S(1)} %bitcast.41, bf16[4096,12,64]{0,2,1:T(8,128)(2,1)} %bitcast.39), kind=kOutput, calls=%fused_computation.2 | convolution fusion | flops 1648358400 | bytes 58077184 | tf_op jit(solution)/shard_map/qhd,khd->hqk/dot_general | solution.py:64
  321.9 23.4 %fusion.1 = f32[12,256]{1,0:T(8,128)S(1)} fusion(f32[12,256,4096]{2,1,0:T(8,128)} %get-tuple-element.76, f32[12,256]{1,0:T(8,128)S(1)} %broadcast_maximum_fusion, pred[256,4096]{1,0:T(8,128)(4,1)S(1)} %broadcast_compare_fusion), kind=kLoop, calls=%fused_computation.3 | loop fusion | flops 62911488 | bytes 51404800 | tf_op jit(solution)/shard_map/reduce_sum | solution.py:76
  345.3 21.8 %fusion.25 = bf16[256,12,64]{0,2,1:T(8,128)(2,1)S(1)} fusion(bf16[4096,12,64]{0,2,1:T(8,128)(2,1)} %bitcast.40, f32[12,256,4096]{2,1,0:T(8,128)} %get-tuple-element.76, f32[12,256]{1,0:T(8,128)S(1)} %broadcast_maximum_fusion, pred[256,4096]{1,0:T(8,128)(4,1)S(1)} %broadcast_compare_fusion, f32[256,12]{0,1:T(8,128)S(1)} %bitcast.45), kind=kOutput, calls=%fused_computation.62 | convolution fusion | flops 1673920512 | bytes 58089472 | tf_op jit(solution)/shard_map/hqk,khd->qhd/dot_general | solution.py:77
  367.2 2.6 fusion.72
  370.1 180.6 %all-gather.11.cloned.1.call-done = bf16[1536,3072]{1,0:T(8,128)(2,1)} async-done(((bf16[96,3072]{1,0:T(8,128)(2,1)}), bf16[1536,3072]{1,0:T(8,128)(2,1)}) %all-gather.11.cloned.1.call-update) | async-done | bytes 9437200 | tf_op jit(solution)/shard_map/all_gather | solution.py:93
  550.7 5.2 fusion.28
  556.4 2.7 collective-permute-start.1
  559.1 5.2 collective-permute-start
  564.6 0.9 collective-permute-done
  565.5 16.3 %fusion.69 = (f32[256]{0:T(256)S(1)}, f32[256,1536]{1,0:T(8,128)S(1)}) fusion(f32[1536]{0:T(1024)S(1)} %get-tuple-element.35, bf16[16,1536]{1,0:T(8,128)(2,1)S(1)} %collective-permute-done.1, bf16[256,1536]{1,0:T(8,128)(2,1)S(1)} %fusion.18, pred[256]{0:T(512)(128)(4,1)S(1)} %get-tuple-element.44, f32[1536]{0:T(1024)S(1)} %get-tuple-element.36, ...), kind=kLoop, calls=%fused_computation.195 | loop fusion | flops 86900480 | bytes 2663424 | tf_op jit(solution)/shard_map/reduce_sum | solution.py:28
  582.1 1.5 fusion.65
  (40 shorter events, 3.7 us)
Async XLA Ops:
  6.5 2.1 copy-start
  6.5 161.9 %copy-start.5 = (f32[1536]{0:T(1024)S(1)}, f32[1536]{0:T(1024)}, u32[]{:S(2)}) copy-start(f32[1536]{0:T(1024)} %param.11) | copy-start | bytes 18436
  6.5 161.9 %all-gather.5.cloned.1.call-start = ((), (), s32[]{:S(2)}) async-start(), calls=%async_computation | async-start | bytes 7520256 | tf_op jit(solution)/shard_map/all_gather | solution.py:48
  7.3 263.5 %all-gather.7.cloned.1.call-start = ((), (), s32[]{:S(2)}) async-start(), calls=%async_computation.1 | async-start | bytes 13369344 | tf_op jit(solution)/shard_map/all_gather | solution.py:55
  173.6 1.1 copy-start.1
  174.7 2.3 copy-start.3
  174.7 24.4 %copy-start.2 = (f32[32,1536]{1,0:T(8,128)S(1)}, f32[32,1536]{1,0:T(8,128)}, u32[]{:S(2)}) copy-start(f32[32,1536]{1,0:T(8,128)} %param.16) | copy-start | bytes 589828
  175.6 191.5 %all-gather.9.cloned.1.call-start = ((), (), s32[]{:S(2)}) async-start(), calls=%async_computation.2 | async-start | bytes 2506752 | tf_op jit(solution)/shard_map/all_gather | solution.py:90
  176.4 374.3 %all-gather.11.cloned.1.call-start = ((), (), s32[]{:S(2)}) async-start(), calls=%async_computation.3 | async-start | bytes 10027008 | tf_op jit(solution)/shard_map/all_gather | solution.py:93
  369.7 180.9 %copy-start.6 = (f32[1536]{0:T(1024)S(1)}, f32[1536]{0:T(1024)}, u32[]{:S(2)}) copy-start(f32[1536]{0:T(1024)} %param.14) | copy-start | bytes 18436
  556.4 8.2 %collective-permute-start.1 = (bf16[16,1536]{1,0:T(8,128)(2,1)S(1)}, bf16[16,1536]{1,0:T(8,128)(2,1)S(1)}, u32[]{:S(2)}, u32[]{:S(2)}) collective-permute-start(bf16[16,1536]{1,0:T(8,128)(2,1)S(1)} %get-tuple-element.42), channel_id=1, source_target_pairs={{1,0},{2,1},{3,2},{4,3},{5,4},{6,5},{7,6},{8,7},{9,8},{10,9},{11,1... | collective-permute-start | bytes 147464 | tf_op jit(solution)/shard_map/ppermute | solution.py:21
  559.1 6.4 %collective-permute-start = (bf16[16,1536]{1,0:T(8,128)(2,1)S(1)}, bf16[16,1536]{1,0:T(8,128)(2,1)S(1)}, u32[]{:S(2)}, u32[]{:S(2)}) collective-permute-start(bf16[16,1536]{1,0:T(8,128)(2,1)S(1)} %get-tuple-element.41), channel_id=1, source_target_pairs={{0,1},{1,2},{2,3},{3,4},{4,5},{5,6},{6,7},{7,8},{8,9},{9,10},{10,1... | collective-permute-start | bytes 147464 | tf_op jit(solution)/shard_map/ppermute | solution.py:18
  565.5 16.6 %copy-start.4 = (f32[1536]{0:T(1024)S(1)}, f32[1536]{0:T(1024)}, u32[]{:S(2)}) copy-start(f32[1536]{0:T(1024)} %param.17) | copy-start | bytes 18436
Sparse Core Ops, SparseCore 0:
  9.1 159.2 all-gather.4
  175.8 94.9 all-gather.6
  272.6 63.7 all-gather.8
  338.0 212.5 all-gather.10
